TPU v7x, 256 devices: a whole 4x4x8 slice. The times are simulated.
256 devices in a mesh: loop: 16 (over z, x_lo), row: 4 (over x_hi, core), col: 4 (over y).
Axes of the slice: x: 4 (x_hi: 2, x_lo: 2; x = x_hi * 2 + x_lo), y: 4, z: 8, core: 2. Of those that a mesh axis runs over, the one named last changes fastest.
Arguments:
- interval_blocks: bfloat16 [16, 4, 2048, 2048], P('loop', None, 'row', 'col'), may hold values from -0.15625 to 0.15625
- interval_pivots: int32 [16, 3, 2048], P('loop'), may hold values from 0 to 2047, each once within a row
- boundary_pivots: int32 [16, 2048], replicated, may hold values from 0 to 2047, each once within a row
- interval_residuals: bfloat16 [16, 4, 2048], P('loop', None, ('row', 'col')), may hold values from -0.23925781 to 0.23925781
Outputs:
- reduced_block: bfloat16 [16, 2048, 2048], P('loop', 'row', 'col')
- reduced_rhs: float32 [16, 2048], P('loop', ('row', 'col'))
Inputs may be any that keep to these rules, and one draw needn't show every extreme that they name: Each row of interval_pivots is a permutation of 0 to 2047. Each row of boundary_pivots is a permutation of 0 to 2047.
All inputs are finite; a program needn't handle non-finite values.
Results may differ from a plain program's by a relative error of at most 0.018.
Values may be sent and summed in bfloat16 or wider, within the bound.
A program may use at most 64 MiB of HBM per device.

v0:
```python
import jax
import jax.numpy as jnp
from jax import lax
from jax.sharding import PartitionSpec as P


def from_behind(value, axis, by):
    devices = lax.axis_size(axis)
    return lax.ppermute(value, axis, [(i, (i + by) % devices) for i in range(devices)])


def compose(left_block, right_block, right_vector, pivots, added):
    column_panel = lax.all_gather(right_block, "row", axis=0, tiled=True)
    full_vector = lax.all_gather(right_vector, ("row", "col"), axis=0, tiled=True)
    permuted = jnp.take(column_panel, pivots, axis=0)
    moved = jnp.take(full_vector, pivots, axis=0)
    segment = lax.all_gather(left_block, "col", axis=1, tiled=True)
    product = jnp.dot(segment, permuted, preferred_element_type=jnp.float32)
    applied = jnp.dot(segment, moved, preferred_element_type=jnp.float32)
    share_size = added.shape[0]
    own_part = lax.dynamic_slice_in_dim(applied, lax.axis_index("col") * share_size, share_size, 0)
    return (product, own_part + added.astype(jnp.float32))


def shards(interval_blocks, interval_pivots, boundary_pivots, interval_residuals):
    blocks = interval_blocks[0]
    pivot_rows = interval_pivots[0]
    residuals = interval_residuals[0]
    matrix = blocks[0]
    vector = residuals[0]
    for interval in range(1, blocks.shape[0]):
        product, applied = compose(
            blocks[interval], matrix, vector, pivot_rows[interval - 1], residuals[interval]
        )
        matrix = product.astype(jnp.bfloat16)
        vector = applied.astype(jnp.bfloat16)
    position = lax.axis_index("loop")
    count_loop = lax.axis_size("loop")
    own_pivots = lax.dynamic_index_in_dim(boundary_pivots, position, 0, keepdims=False)
    back_pivots = lax.dynamic_index_in_dim(
        boundary_pivots, (position + count_loop - 1) % count_loop, 0, keepdims=False
    )
    earlier, earlier_vector = from_behind((matrix, vector), "loop", 1)
    product, applied = compose(matrix, earlier, earlier_vector, own_pivots, vector)
    halved = product.astype(jnp.bfloat16)
    halved_vector = applied.astype(jnp.bfloat16)
    distant, distant_vector = from_behind((halved, halved_vector), "loop", 2)
    reduced, reduced_vector = compose(halved, distant, distant_vector, back_pivots, halved_vector)
    return (reduced.astype(jnp.bfloat16)[None], reduced_vector[None])


def solution(mesh):
    placed = (
        P("loop", None, "row", "col"),
        P("loop", None, None),
        P(),
        P("loop", None, ("row", "col")),
    )
    return jax.shard_map(
        shards,
        mesh=mesh,
        in_specs=placed,
        out_specs=(P("loop", "row", "col"), P("loop", ("row", "col"))),
        check_vma=False,
    )
```

profile of v0, /device:TPU:8, one launch (start us, length us, event | category | flops | bytes accessed | tf_op | source)
XLA Modules:
  0.0 394.3 jit_solution(15672747446238209155)
XLA Ops:
  7.2 2.9 fusion.83
  10.2 0.7 all-gather.34.cloned.1.call-update
  10.9 34.3 %all-gather.4 = bf16[1,1,2048]{2,1,0:T(2,128)(2,1)S(1)} all-gather(bf16[1,1,128]{2,1,0:T(2,128)(2,1)S(1)} %slice.51), channel_id=6, replica_groups=mesh['loop'=16,'row'=4,'col'=4] {'row','col'}, dimensions={2}, use_global_device_ids=true | all-gather | bytes 4352 | tf_op jit(solution)/shard_map/all_gather | solution.py:14
  45.3 13.1 %gather_fusion.5 = bf16[2048]{0:T(1024)(128)(2,1)S(1)} fusion(bf16[2048]{0:T(1024)(128)(2,1)S(1)} %reduce, s32[2048]{0:T(1024)S(1)} %fusion.68), kind=kCustom, calls=%fused_computation.1.clone | custom fusion | bytes 16384 | tf_op jit(solution)/shard_map/jit(_take)/gather | solution.py:16
  58.5 9.5 %gather_fusion = bf16[2048,512]{1,0:T(8,128)(2,1)S(1)} fusion(bf16[2048,512]{1,0:T(8,128)(2,1)} %bitcast.80, s32[2048]{0:T(1024)S(1)} %fusion.68), kind=kCustom, calls=%fused_computation.clone | custom fusion | bytes 4202496 | tf_op jit(solution)/shard_map/jit(_take)/gather | solution.py:15
  67.9 8.3 %all-gather.34.cloned.1.call-done = bf16[1,1,512,2048]{3,2,1,0:T(8,128)(2,1)} async-done(((bf16[1,1,512,512]{3,2,1,0:T(8,128)(2,1)}), bf16[1,1,512,2048]{3,2,1,0:T(8,128)(2,1)}) %all-gather.34.cloned.1.call-update) | async-done | bytes 2097168 | tf_op jit(solution)/shard_map/all_gather | solution.py:17
  76.3 4.1 %fusion.55 = bf16[512,512]{0,1:T(8,128)(2,1)} fusion(bf16[1,1,512,2048]{3,2,1,0:T(8,128)(2,1)} %all-gather.34.cloned.1.call-done, bf16[2048,512]{1,0:T(8,128)(2,1)S(1)} %gather_fusion, pred[2048]{0:T(1024)(128)(4,1)S(1)} %get-tuple-element.13), kind=kOutput, calls=%fused_computation.41 | convolution fusion | flops 1075052544 | bytes 4720640 | tf_op jit(solution)/shard_map/dot_general | solution.py:18
  80.4 0.5 all-gather.36.cloned.1.call-update
  81.0 2.2 fusion.8
  83.2 0.1 fusion.77
  83.3 33.7 %all-gather.5 = bf16[16,1,128]{2,1,0:T(2,128)(2,1)S(1)} all-gather(bf16[1,1,128]{2,1,0:T(2,128)(2,1)S(1)} %fusion.77), channel_id=1, replica_groups=mesh['loop'=16,'row'=4,'col'=4] {'row','col'}, dimensions={0}, use_global_device_ids=true | all-gather | bytes 4352 | tf_op jit(solution)/shard_map/all_gather | solution.py:14
  117.0 13.1 %gather_fusion.6 = bf16[2048]{0:T(1024)(128)(2,1)S(1)} fusion(bf16[2048]{0:T(1024)(128)(2,1)S(1)} %bitcast.77, s32[2048]{0:T(1024)S(1)} %fusion.69), kind=kCustom, calls=%fused_computation.6.clone | custom fusion | bytes 16384 | tf_op jit(solution)/shard_map/jit(_take)/gather | solution.py:16
  130.1 2.9 copy.8
  133.0 9.2 %gather_fusion.1 = bf16[2048,512]{1,0:T(8,128)(2,1)} fusion(bf16[2048,512]{1,0:T(8,128)(2,1)S(1)} %copy.8, s32[2048]{0:T(1024)S(1)} %fusion.69), kind=kCustom, calls=%fused_computation.2.clone | custom fusion | bytes 4202496 | tf_op jit(solution)/shard_map/jit(_take)/gather | solution.py:15
  142.2 2.1 all-gather.36.cloned.1.call-done
  144.3 4.8 %fusion.50 = bf16[512,512]{0,1:T(8,128)(2,1)} fusion(bf16[1,1,512,2048]{3,2,1,0:T(8,128)(2,1)} %all-gather.36.cloned.1.call-done, bf16[2048,512]{1,0:T(8,128)(2,1)} %gather_fusion.1, pred[2048]{0:T(1024)(128)(4,1)S(1)} %get-tuple-element.11), kind=kOutput, calls=%fused_computation.40 | convolution fusion | flops 1075052544 | bytes 4720640 | tf_op jit(solution)/shard_map/dot_general | solution.py:18
  149.2 0.5 all-gather.38.cloned.1.call-update
  149.8 0.6 fusion.4
  150.4 0.1 fusion.75
  150.5 33.7 %all-gather.6 = bf16[16,1,128]{2,1,0:T(2,128)(2,1)S(1)} all-gather(bf16[1,1,128]{2,1,0:T(2,128)(2,1)S(1)} %fusion.75), channel_id=1, replica_groups=mesh['loop'=16,'row'=4,'col'=4] {'row','col'}, dimensions={0}, use_global_device_ids=true | all-gather | bytes 4352 | tf_op jit(solution)/shard_map/all_gather | solution.py:14
  184.2 13.1 %gather_fusion.7 = bf16[2048]{0:T(1024)(128)(2,1)S(1)} fusion(bf16[2048]{0:T(1024)(128)(2,1)S(1)} %bitcast.78, s32[2048]{0:T(1024)S(1)} %fusion.70), kind=kCustom, calls=%fused_computation.7.clone | custom fusion | bytes 16384 | tf_op jit(solution)/shard_map/jit(_take)/gather | solution.py:16
  197.4 2.9 copy.9
  200.2 9.2 %gather_fusion.2 = bf16[2048,512]{1,0:T(8,128)(2,1)} fusion(bf16[2048,512]{1,0:T(8,128)(2,1)S(1)} %copy.9, s32[2048]{0:T(1024)S(1)} %fusion.70), kind=kCustom, calls=%fused_computation.3.clone | custom fusion | bytes 4202496 | tf_op jit(solution)/shard_map/jit(_take)/gather | solution.py:15
  209.4 3.7 all-gather.38.cloned.1.call-done
  213.1 4.0 %fusion.45 = bf16[512,512]{0,1:T(8,128)(2,1)S(1)} fusion(bf16[1,1,512,2048]{3,2,1,0:T(8,128)(2,1)} %all-gather.38.cloned.1.call-done, bf16[2048,512]{1,0:T(8,128)(2,1)} %gather_fusion.2, pred[2048]{0:T(1024)(128)(4,1)S(1)} %get-tuple-element.9), kind=kOutput, calls=%fused_computation.39 | convolution fusion | flops 1075052544 | bytes 4720640 | tf_op jit(solution)/shard_map/dot_general | solution.py:18
  217.1 1.5 collective-permute-start
  218.7 14.7 %collective-permute-done = bf16[512,512]{0,1:T(8,128)(2,1)S(1)} collective-permute-done((bf16[512,512]{0,1:T(8,128)(2,1)S(1)}, bf16[512,512]{0,1:T(8,128)(2,1)S(1)}, u32[]{:S(2)}, u32[]{:S(2)}) %collective-permute-start) | collective-permute-done | bytes 524320 | tf_op jit(solution)/shard_map/ppermute | solution.py:9
  233.4 0.8 copy-done.4
  234.3 0.7 all-gather.24.cloned.1.call-update
  235.0 0.9 constant_dynamic-slice_fusion
  235.9 0.6 fusion
  236.7 0.2 collective-permute-start.2
  236.9 5.6 %collective-permute-done.2 = bf16[128]{0:T(256)(128)(2,1)S(1)} collective-permute-done((bf16[128]{0:T(256)(128)(2,1)S(1)}, bf16[128]{0:T(256)(128)(2,1)S(1)}, u32[]{:S(2)}, u32[]{:S(2)}) %collective-permute-start.2) | collective-permute-done | bytes 288 | tf_op jit(solution)/shard_map/ppermute | solution.py:9
  242.5 33.6 %all-gather.7 = bf16[16,1,128]{2,1,0:T(2,128)(2,1)S(1)} all-gather(bf16[1,1,128]{2,1,0:T(2,128)(2,1)S(1)} %bitcast.97), channel_id=1, replica_groups=mesh['loop'=16,'row'=4,'col'=4] {'row','col'}, dimensions={0}, use_global_device_ids=true | all-gather | bytes 4352 | tf_op jit(solution)/shard_map/all_gather | solution.py:14
  276.2 13.1 %gather_fusion.8 = bf16[2048]{0:T(1024)(128)(2,1)S(1)} fusion(bf16[2048]{0:T(1024)(128)(2,1)S(1)} %bitcast.79, s32[2048]{0:T(1024)S(1)} %fusion.71), kind=kCustom, calls=%fused_computation.8.clone | custom fusion | bytes 16384 | tf_op jit(solution)/shard_map/jit(_take)/gather | solution.py:16
  289.3 2.9 copy.10
  292.2 9.2 %gather_fusion.3 = bf16[2048,512]{1,0:T(8,128)(2,1)} fusion(bf16[2048,512]{1,0:T(8,128)(2,1)S(1)} %copy.10, s32[2048]{0:T(1024)S(1)} %fusion.71), kind=kCustom, calls=%fused_computation.4.clone | custom fusion | bytes 4202496 | tf_op jit(solution)/shard_map/jit(_take)/gather | solution.py:15
  301.4 4.5 %fusion.24 = bf16[512,512]{1,0:T(8,128)(2,1)} fusion(bf16[512,2048]{0,1:T(8,128)(2,1)} %all-gather.24.cloned.1.call-done, bf16[2048,512]{1,0:T(8,128)(2,1)} %gather_fusion.3, pred[2048]{0:T(1024)(128)(4,1)S(1)} %get-tuple-element.7), kind=kOutput, calls=%fused_computation.34 | convolution fusion | flops 1075052544 | bytes 4720640 | tf_op jit(solution)/shard_map/dot_general | solution.py:18
  306.1 12.5 %collective-permute-done.1 = bf16[512,512]{1,0:T(8,128)(2,1)S(1)} collective-permute-done((bf16[512,512]{1,0:T(8,128)(2,1)}, bf16[512,512]{1,0:T(8,128)(2,1)S(1)}, u32[]{:S(2)}, u32[]{:S(2)}) %collective-permute-start.1) | collective-permute-done | bytes 524320 | tf_op jit(solution)/shard_map/ppermute | solution.py:9
  318.6 0.8 copy-done.5
  319.4 0.4 fusion.85
  319.9 4.7 %collective-permute-done.3 = bf16[128]{0:T(256)(128)(2,1)S(1)} collective-permute-done((bf16[128]{0:T(256)(128)(2,1)S(1)}, bf16[128]{0:T(256)(128)(2,1)S(1)}, u32[]{:S(2)}, u32[]{:S(2)}) %collective-permute-start.3) | collective-permute-done | bytes 288 | tf_op jit(solution)/shard_map/ppermute | solution.py:9
  324.7 33.6 %all-gather.8 = bf16[16,1,128]{2,1,0:T(2,128)(2,1)S(1)} all-gather(bf16[1,1,128]{2,1,0:T(2,128)(2,1)S(1)} %bitcast.96), channel_id=1, replica_groups=mesh['loop'=16,'row'=4,'col'=4] {'row','col'}, dimensions={0}, use_global_device_ids=true | all-gather | bytes 4352 | tf_op jit(solution)/shard_map/all_gather | solution.py:14
  358.3 13.1 %gather_fusion.9 = bf16[2048]{0:T(1024)(128)(2,1)S(1)} fusion(bf16[2048]{0:T(1024)(128)(2,1)S(1)} %bitcast.76, s32[2048]{0:T(1024)S(1)} %fusion.72), kind=kCustom, calls=%fused_computation.9.clone | custom fusion | bytes 16384 | tf_op jit(solution)/shard_map/jit(_take)/gather | solution.py:16
  371.5 2.2 fusion.86
  373.7 0.6 add_bitcast_fusion
  374.3 9.4 %gather_fusion.4 = bf16[2048,512]{1,0:T(8,128)(2,1)S(1)} fusion(bf16[2048,512]{1,0:T(8,128)(2,1)} %all-gather.30.cloned.1.call-done, s32[2048]{0:T(1024)S(1)} %fusion.72), kind=kCustom, calls=%fused_computation.5.clone | custom fusion | bytes 4202496 | tf_op jit(solution)/shard_map/jit(_take)/gather | solution.py:15
  383.8 3.7 fusion.60
  (63 shorter events, 1.2 us)
Async XLA Ops:
  7.2 3.7 copy-start.7
  7.2 38.1 %copy-start.6 = (s32[1,3,2048]{2,0,1:T(1,128)S(1)}, s32[1,3,2048]{2,0,1:T(1,128)}, u32[]{:S(2)}) copy-start(s32[1,3,2048]{2,0,1:T(1,128)} %param.9) | copy-start | bytes 73732
  7.2 51.3 %all-gather.32.cloned.1.call-start = ((), (), s32[]{:S(2)}) async-start(), calls=%async_computation.6 | async-start | bytes 2621440 | tf_op jit(solution)/shard_map/all_gather | solution.py:13
  10.1 66.1 %all-gather.34.cloned.1.call-start = ((), (), s32[]{:S(2)}) async-start(), calls=%async_computation.7 | async-start | bytes 2621440 | tf_op jit(solution)/shard_map/all_gather | solution.py:17
  10.9 119.3 %all-gather.20.cloned.1.call-start = ((), (), s32[]{:S(2)}) async-start(), calls=%async_computation | async-start | bytes 2621440 | tf_op jit(solution)/shard_map/all_gather | solution.py:13
  80.3 63.9 %all-gather.36.cloned.1.call-start = ((), (), s32[]{:S(2)}) async-start(), calls=%async_computation.8 | async-start | bytes 2621440 | tf_op jit(solution)/shard_map/all_gather | solution.py:17
  80.9 116.4 %all-gather.22.cloned.1.call-start = ((), (), s32[]{:S(2)}) async-start(), calls=%async_computation.1 | async-start | bytes 2621440 | tf_op jit(solution)/shard_map/all_gather | solution.py:13
  144.3 5.5 %copy-start.2 = (bf16[1,1,512,2048]{3,2,1,0:T(8,128)(2,1)S(1)}, bf16[1,1,512,2048]{3,2,1,0:T(8,128)(2,1)}, u32[]{:S(2)}) copy-start(bf16[1,1,512,2048]{3,2,1,0:T(8,128)(2,1)} %all-gather.36.cloned.1.call-done) | copy-start | bytes 6291460
  149.1 63.9 %all-gather.38.cloned.1.call-start = ((), (), s32[]{:S(2)}) async-start(), calls=%async_computation.9 | async-start | bytes 2621440 | tf_op jit(solution)/shard_map/all_gather | solution.py:17
  149.7 139.6 %all-gather.26.cloned.1.call-start = ((), (), s32[]{:S(2)}) async-start(), calls=%async_computation.3 | async-start | bytes 2621440 | tf_op jit(solution)/shard_map/all_gather | solution.py:13
  213.1 22.8 %copy-start.1 = (bf16[1,1,512,2048]{3,2,1,0:T(8,128)(2,1)S(1)}, bf16[1,1,512,2048]{3,2,1,0:T(8,128)(2,1)}, u32[]{:S(2)}) copy-start(bf16[1,1,512,2048]{3,2,1,0:T(8,128)(2,1)} %all-gather.38.cloned.1.call-done) | copy-start | bytes 6291460
  217.1 17.1 %copy-start.3 = (bf16[512,512]{0,1:T(8,128)(2,1)}, bf16[512,512]{0,1:T(8,128)(2,1)S(1)}, u32[]{:S(2)}) copy-start(bf16[512,512]{0,1:T(8,128)(2,1)S(1)} %fusion.45) | copy-start | bytes 1572868
  217.1 16.2 %collective-permute-start = (bf16[512,512]{0,1:T(8,128)(2,1)S(1)}, bf16[512,512]{0,1:T(8,128)(2,1)S(1)}, u32[]{:S(2)}, u32[]{:S(2)}) collective-permute-start(bf16[512,512]{0,1:T(8,128)(2,1)S(1)} %fusion.45), channel_id=1, source_target_pairs={{0,16},{16,32},{32,48},{48,64},{64,80},{80,96},{96,112},{112,128},... | collective-permute-start | bytes 1572872 | tf_op jit(solution)/shard_map/ppermute | solution.py:9
  233.4 0.8 copy-start.4
  234.2 67.2 %all-gather.24.cloned.1.call-start = ((), (), s32[]{:S(2)}) async-start(), calls=%async_computation.2 | async-start | bytes 2621440 | tf_op jit(solution)/shard_map/all_gather | solution.py:17
  235.0 136.5 %all-gather.28.cloned.1.call-start = ((), (), s32[]{:S(2)}) async-start(), calls=%async_computation.4 | async-start | bytes 2621440 | tf_op jit(solution)/shard_map/all_gather | solution.py:17
  236.7 5.8 %collective-permute-start.2 = (bf16[128]{0:T(256)(128)(2,1)S(1)}, bf16[128]{0:T(256)(128)(2,1)S(1)}, u32[]{:S(2)}, u32[]{:S(2)}) collective-permute-start(bf16[128]{0:T(256)(128)(2,1)S(1)} %fusion.73), channel_id=1, source_target_pairs={{0,16},{16,32},{32,48},{48,64},{64,80},{80,96},{96,112},{112,128},... | collective-permute-start | bytes 776 | tf_op jit(solution)/shard_map/ppermute | solution.py:9
  301.4 18.0 %copy-start = (bf16[512,2048]{0,1:T(8,128)(2,1)S(1)}, bf16[512,2048]{0,1:T(8,128)(2,1)}, u32[]{:S(2)}) copy-start(bf16[512,2048]{0,1:T(8,128)(2,1)} %all-gather.24.cloned.1.call-done) | copy-start | bytes 6291460
  305.9 68.4 %all-gather.30.cloned.1.call-start = ((), (), s32[]{:S(2)}) async-start(), calls=%async_computation.5 | async-start | bytes 2621440 | tf_op jit(solution)/shard_map/all_gather | solution.py:13
  306.0 12.6 %collective-permute-start.1 = (bf16[512,512]{1,0:T(8,128)(2,1)}, bf16[512,512]{1,0:T(8,128)(2,1)S(1)}, u32[]{:S(2)}, u32[]{:S(2)}) collective-permute-start(bf16[512,512]{1,0:T(8,128)(2,1)} %fusion.24), channel_id=1, source_target_pairs={{0,32},{16,48},{32,64},{48,80},{64,96},{80,112},{96,128},{112,144}... | collective-permute-start | bytes 1572872 | tf_op jit(solution)/shard_map/ppermute | solution.py:9
  318.6 0.8 copy-start.5
  319.9 4.8 %collective-permute-start.3 = (bf16[128]{0:T(256)(128)(2,1)S(1)}, bf16[128]{0:T(256)(128)(2,1)S(1)}, u32[]{:S(2)}, u32[]{:S(2)}) collective-permute-start(bf16[128]{0:T(256)(128)(2,1)S(1)} %add_convert_fusion), channel_id=1, source_target_pairs={{0,32},{16,48},{32,64},{48,80},{64,96},{80,112},{96,128},{112,144}... | collective-permute-start | bytes 776 | tf_op jit(solution)/shard_map/ppermute | solution.py:9
Sparse Core Ops, SparseCore 0:
  10.4 32.0 all-gather.31
  44.3 31.9 all-gather.33
  80.5 30.1 all-gather.19
  112.3 31.9 all-gather.35
  149.3 30.1 all-gather.21
  181.1 31.9 all-gather.37
  234.3 29.7 all-gather.25
  266.5 31.9 all-gather.23
  306.0 31.8 all-gather.27
  339.6 30.1 all-gather.29
where the time goes:
time: 395 us; the launch traced here: 394 us
  blocking collectives  169 us (43%)
  local copies, waits for them, and re-layouts  126 us (32%)
  waiting for transfers between devices  54.3 us (14%)
  matrix products  27.2 us (7%)
  between operations  14.6 us (4%)
    all_gather x5, blocking collectives, compose(): lax.all_gather(right_vector, ('row', 'col'), axis=0, tiled=True)  169 us
    gather x5, local copies, waits for them, and re-layouts, compose(): moved = jnp.take(full_vector, pivots, axis=0)  65.4 us
    gather x5, local copies, waits for them, and re-layouts, compose(): permuted = jnp.take(column_panel, pivots, axis=0)  46.4 us
    ppermute x4, waiting for transfers between devices, from_behind(): lax.ppermute(value, axis, [(i, (i + by) % devices) for i in range(devices)])  37.5 us
    dot_general x5, matrix products, compose(): product = jnp.dot(segment, permuted, preferred_element_type=jnp.float32)  21.1 us
    all_gather x5, waiting for transfers between devices, compose(): segment = lax.all_gather(left_block, 'col', axis=1, tiled=True)  14.1 us
    all_gather x3, local copies, waits for them, and re-layouts, compose(): column_panel = lax.all_gather(right_block, 'row', axis=0, tiled=True)  8.65 us
  transfers between devices with their start and end apart: 14, of which 7 were waited for; matrix products, arithmetic and copies ran while one was open for 30% of the time, Pallas kernels for 0%

commit v1 on v0

--- a/solution.py
+++ b/solution.py
@@ -14,7 +14,9 @@
     full_vector = lax.all_gather(right_vector, ("row", "col"), axis=0, tiled=True)
     permuted = jnp.take(column_panel, pivots, axis=0)
     moved = jnp.take(full_vector, pivots, axis=0)
-    segment = lax.all_gather(left_block, "col", axis=1, tiled=True)
+    segment = jnp.concatenate(
+        lax.all_to_all(jnp.stack([left_block] * lax.axis_size("col")), "col", 0, 0), axis=1
+    )
     product = jnp.dot(segment, permuted, preferred_element_type=jnp.float32)
     applied = jnp.dot(segment, moved, preferred_element_type=jnp.float32)
     share_size = added.shape[0]

time: 395 us -> 466 us (1.18)
  blocking collectives: 169 us -> 222 us
  starting transfers between devices: 2.26 us -> 31 us
  waiting for transfers between devices: 54.3 us -> 33.2 us
  local copies, waits for them, and re-layouts: 126 us -> 138 us
    all_gather x5, blocking collectives: 169 us -> 222 us  [compose(): lax.all_gather(right_vector, ('row', 'col'), axis=0, tiled=True)]
    all_to_all x0 -> x5, starting transfers between devices: none -> 30.1 us  [compose(): lax.all_to_all(jnp.stack([left_block] * lax.axis_size('col')), 'col', 0, 0)]
    all_gather x5 -> x0, waiting for transfers between devices: 14.1 us -> none  [compose(): segment = lax.all_gather(left_block, 'col', axis=1, tiled=True)]
    another operation x0 -> x5, local copies, waits for them, and re-layouts: none -> 7.57 us  [compose(): jnp.stack([left_block] * lax.axis_size('col'))]
  transfers between devices with their start and end apart: 14 -> 14, of which waited for: 7 -> 4; matrix products, arithmetic and copies ran while one was open for 30% -> 28% of each run, Pallas kernels for 0% -> 0%
where the time goes in v1:
time: 466 us; the launch traced here: 465 us
  blocking collectives  222 us (48%)
  local copies, waits for them, and re-layouts  138 us (30%)
  waiting for transfers between devices  33.2 us (7%)
  starting transfers between devices  31 us (7%)
  matrix products  25.7 us (6%)
  between operations  14.1 us (3%)
    all_gather x5, blocking collectives, compose(): lax.all_gather(right_vector, ('row', 'col'), axis=0, tiled=True)  222 us
    gather x5, local copies, waits for them, and re-layouts, compose(): moved = jnp.take(full_vector, pivots, axis=0)  65.4 us
    gather x5, local copies, waits for them, and re-layouts, compose(): permuted = jnp.take(column_panel, pivots, axis=0)  49.8 us
    ppermute x4, waiting for transfers between devices, from_behind(): lax.ppermute(value, axis, [(i, (i + by) % devices) for i in range(devices)])  33.1 us
    all_to_all x5, starting transfers between devices, compose(): lax.all_to_all(jnp.stack([left_block] * lax.axis_size('col')), 'col', 0, 0)  30.1 us
    dot_general x5, matrix products, compose(): product = jnp.dot(segment, permuted, preferred_element_type=jnp.float32)  19.1 us
  transfers between devices with their start and end apart: 14, of which 4 were waited for; matrix products, arithmetic and copies ran while one was open for 28% of the time, Pallas kernels for 0%

profile of v1, /device:TPU:8, one launch (start us, length us, event | category | flops | bytes accessed | tf_op | source)
XLA Modules:
  0.0 465.3 jit_solution(10889544716544651311)
XLA Ops:
  7.2 2.7 fusion.62
  10.1 1.5 stack.10
  11.6 5.9 %all-to-all-start = ((bf16[4,512,512]{1,2,0:T(8,128)(2,1)}), bf16[4,512,512]{1,2,0:T(8,128)(2,1)S(1)}, u32[]{:S(2)}, u32[]{:S(2)}) async-start(bf16[4,512,512]{1,2,0:T(8,128)(2,1)} %stack.10), calls=%async_computation | async-start | bytes 4194304 | tf_op jit(solution)/shard_map/all_to_all | solution.py:18
  17.5 48.9 %all-gather.1 = bf16[1,1,2048]{2,1,0:T(2,128)(2,1)S(1)} all-gather(bf16[1,1,128]{2,1,0:T(2,128)(2,1)S(1)} %slice.60), channel_id=3, replica_groups=mesh['loop'=16,'row'=4,'col'=4] {'row','col'}, dimensions={2}, use_global_device_ids=true | all-gather | bytes 4352 | tf_op jit(solution)/shard_map/all_gather | solution.py:14
  66.4 13.1 %gather_fusion.5 = bf16[2048]{0:T(1024)(128)(2,1)S(1)} fusion(bf16[2048]{0:T(1024)(128)(2,1)S(1)} %reduce, s32[2048]{0:T(1024)S(1)} %fusion.47), kind=kCustom, calls=%fused_computation.1.clone | custom fusion | bytes 16384 | tf_op jit(solution)/shard_map/jit(_take)/gather | solution.py:16
  79.6 11.1 %gather_fusion = bf16[2048,512]{1,0:T(8,128)(2,1)} fusion(bf16[2048,512]{1,0:T(8,128)(2,1)} %bitcast.80, s32[2048]{0:T(1024)S(1)} %fusion.47), kind=kCustom, calls=%fused_computation.clone | custom fusion | bytes 4202496 | tf_op jit(solution)/shard_map/jit(_take)/gather | solution.py:15
  90.7 3.8 fusion.39
  94.5 1.3 copy.15
  95.8 1.5 stack.11
  97.3 6.9 %all-to-all-start.1 = ((bf16[4,512,512]{1,2,0:T(8,128)(2,1)}), bf16[4,512,512]{1,2,0:T(8,128)(2,1)}, u32[]{:S(2)}, u32[]{:S(2)}) async-start(bf16[4,512,512]{1,2,0:T(8,128)(2,1)} %stack.11), calls=%async_computation.1 | async-start | bytes 4194304 | tf_op jit(solution)/shard_map/all_to_all | solution.py:18
  104.7 44.8 %all-gather.2 = bf16[16,1,128]{2,1,0:T(2,128)(2,1)S(1)} all-gather(bf16[1,1,128]{2,1,0:T(2,128)(2,1)S(1)} %fusion.56), channel_id=1, replica_groups=mesh['loop'=16,'row'=4,'col'=4] {'row','col'}, dimensions={0}, use_global_device_ids=true | all-gather | bytes 4352 | tf_op jit(solution)/shard_map/all_gather | solution.py:14
  149.5 13.1 %gather_fusion.6 = bf16[2048]{0:T(1024)(128)(2,1)S(1)} fusion(bf16[2048]{0:T(1024)(128)(2,1)S(1)} %bitcast.77, s32[2048]{0:T(1024)S(1)} %fusion.48), kind=kCustom, calls=%fused_computation.6.clone | custom fusion | bytes 16384 | tf_op jit(solution)/shard_map/jit(_take)/gather | solution.py:16
  162.7 2.9 copy.14
  165.5 9.2 %gather_fusion.1 = bf16[2048,512]{1,0:T(8,128)(2,1)} fusion(bf16[2048,512]{1,0:T(8,128)(2,1)S(1)} %copy.14, s32[2048]{0:T(1024)S(1)} %fusion.48), kind=kCustom, calls=%fused_computation.2.clone | custom fusion | bytes 4202496 | tf_op jit(solution)/shard_map/jit(_take)/gather | solution.py:15
  174.7 4.4 fusion.36
  179.4 1.5 stack.12
  180.9 4.7 %all-to-all-start.2 = ((bf16[4,512,512]{1,2,0:T(8,128)(2,1)}), bf16[4,512,512]{1,2,0:T(8,128)(2,1)}, u32[]{:S(2)}, u32[]{:S(2)}) async-start(bf16[4,512,512]{1,2,0:T(8,128)(2,1)} %stack.12), calls=%async_computation.2 | async-start | bytes 4194304 | tf_op jit(solution)/shard_map/all_to_all | solution.py:18
  185.6 2.0 fusion.65
  187.7 44.3 %all-gather.3 = bf16[16,1,128]{2,1,0:T(2,128)(2,1)S(1)} all-gather(bf16[1,1,128]{2,1,0:T(2,128)(2,1)S(1)} %fusion.54), channel_id=1, replica_groups=mesh['loop'=16,'row'=4,'col'=4] {'row','col'}, dimensions={0}, use_global_device_ids=true | all-gather | bytes 4352 | tf_op jit(solution)/shard_map/all_gather | solution.py:14
  232.0 13.1 %gather_fusion.7 = bf16[2048]{0:T(1024)(128)(2,1)S(1)} fusion(bf16[2048]{0:T(1024)(128)(2,1)S(1)} %bitcast.78, s32[2048]{0:T(1024)S(1)} %fusion.49), kind=kCustom, calls=%fused_computation.7.clone | custom fusion | bytes 16384 | tf_op jit(solution)/shard_map/jit(_take)/gather | solution.py:16
  245.2 2.9 copy.16
  248.0 9.2 %gather_fusion.2 = bf16[2048,512]{1,0:T(8,128)(2,1)} fusion(bf16[2048,512]{1,0:T(8,128)(2,1)S(1)} %copy.16, s32[2048]{0:T(1024)S(1)} %fusion.49), kind=kCustom, calls=%fused_computation.3.clone | custom fusion | bytes 4202496 | tf_op jit(solution)/shard_map/jit(_take)/gather | solution.py:15
  257.2 3.6 fusion.33
  260.9 0.8 collective-permute-start
  261.6 12.3 %collective-permute-done = bf16[512,512]{0,1:T(8,128)(2,1)S(1)} collective-permute-done((bf16[512,512]{0,1:T(8,128)(2,1)S(1)}, bf16[512,512]{0,1:T(8,128)(2,1)S(1)}, u32[]{:S(2)}, u32[]{:S(2)}) %collective-permute-start) | collective-permute-done | bytes 524320 | tf_op jit(solution)/shard_map/ppermute | solution.py:9
  274.0 0.8 copy-done
  274.8 1.5 stack.26
  276.3 5.8 %all-to-all-start.3 = ((bf16[4,512,512]{1,2,0:T(8,128)(2,1)}), bf16[4,512,512]{1,2,0:T(8,128)(2,1)}, u32[]{:S(2)}, u32[]{:S(2)}) async-start(bf16[4,512,512]{1,2,0:T(8,128)(2,1)} %stack.26), calls=%async_computation.3 | async-start | bytes 4194304 | tf_op jit(solution)/shard_map/all_to_all | solution.py:18
  282.2 0.9 constant_dynamic-slice_fusion
  283.1 2.0 fusion.66
  285.2 5.6 %collective-permute-done.2 = bf16[128]{0:T(256)(128)(2,1)S(1)} collective-permute-done((bf16[128]{0:T(256)(128)(2,1)S(1)}, bf16[128]{0:T(256)(128)(2,1)S(1)}, u32[]{:S(2)}, u32[]{:S(2)}) %collective-permute-start.2) | collective-permute-done | bytes 288 | tf_op jit(solution)/shard_map/ppermute | solution.py:9
  290.8 40.5 %all-gather.4 = bf16[16,1,128]{2,1,0:T(2,128)(2,1)S(1)} all-gather(bf16[1,1,128]{2,1,0:T(2,128)(2,1)S(1)} %bitcast.101), channel_id=1, replica_groups=mesh['loop'=16,'row'=4,'col'=4] {'row','col'}, dimensions={0}, use_global_device_ids=true | all-gather | bytes 4352 | tf_op jit(solution)/shard_map/all_gather | solution.py:14
  331.3 13.1 %gather_fusion.8 = bf16[2048]{0:T(1024)(128)(2,1)S(1)} fusion(bf16[2048]{0:T(1024)(128)(2,1)S(1)} %bitcast.79, s32[2048]{0:T(1024)S(1)} %fusion.50), kind=kCustom, calls=%fused_computation.8.clone | custom fusion | bytes 16384 | tf_op jit(solution)/shard_map/jit(_take)/gather | solution.py:16
  344.4 2.9 copy.18
  347.3 9.2 %gather_fusion.3 = bf16[2048,512]{1,0:T(8,128)(2,1)} fusion(bf16[2048,512]{1,0:T(8,128)(2,1)S(1)} %copy.18, s32[2048]{0:T(1024)S(1)} %fusion.50), kind=kCustom, calls=%fused_computation.4.clone | custom fusion | bytes 4202496 | tf_op jit(solution)/shard_map/jit(_take)/gather | solution.py:15
  356.5 3.5 fusion.24
  360.1 10.4 %collective-permute-done.1 = bf16[512,512]{1,0:T(8,128)(2,1)S(1)} collective-permute-done((bf16[512,512]{1,0:T(8,128)(2,1)S(1)}, bf16[512,512]{1,0:T(8,128)(2,1)S(1)}, u32[]{:S(2)}, u32[]{:S(2)}) %collective-permute-start.1) | collective-permute-done | bytes 524320 | tf_op jit(solution)/shard_map/ppermute | solution.py:9
  370.5 0.8 copy-done.1
  371.5 1.5 stack.27
  373.0 6.8 %all-to-all-start.4 = ((bf16[4,512,512]{1,2,0:T(8,128)(2,1)}), bf16[4,512,512]{1,2,0:T(8,128)(2,1)S(1)}, u32[]{:S(2)}, u32[]{:S(2)}) async-start(bf16[4,512,512]{1,2,0:T(8,128)(2,1)} %stack.27), calls=%async_computation.4 | async-start | bytes 4194304 | tf_op jit(solution)/shard_map/all_to_all | solution.py:18
  379.8 2.0 fusion.67
  381.9 4.7 %collective-permute-done.3 = bf16[128]{0:T(256)(128)(2,1)S(1)} collective-permute-done((bf16[128]{0:T(256)(128)(2,1)S(1)}, bf16[128]{0:T(256)(128)(2,1)S(1)}, u32[]{:S(2)}, u32[]{:S(2)}) %collective-permute-start.3) | collective-permute-done | bytes 288 | tf_op jit(solution)/shard_map/ppermute | solution.py:9
  386.6 43.2 %all-gather.5 = bf16[16,1,128]{2,1,0:T(2,128)(2,1)S(1)} all-gather(bf16[1,1,128]{2,1,0:T(2,128)(2,1)S(1)} %bitcast.100), channel_id=1, replica_groups=mesh['loop'=16,'row'=4,'col'=4] {'row','col'}, dimensions={0}, use_global_device_ids=true | all-gather | bytes 4352 | tf_op jit(solution)/shard_map/all_gather | solution.py:14
  429.8 13.1 %gather_fusion.9 = bf16[2048]{0:T(1024)(128)(2,1)S(1)} fusion(bf16[2048]{0:T(1024)(128)(2,1)S(1)} %bitcast.76, s32[2048]{0:T(1024)S(1)} %fusion.51), kind=kCustom, calls=%fused_computation.9.clone | custom fusion | bytes 16384 | tf_op jit(solution)/shard_map/jit(_take)/gather | solution.py:16
  443.0 0.4 fusion.68
  443.3 0.6 add_bitcast_fusion
  443.9 11.1 %gather_fusion.4 = bf16[2048,512]{1,0:T(8,128)(2,1)} fusion(bf16[2048,512]{1,0:T(8,128)(2,1)} %all-gather.18.cloned.1.call-done, s32[2048]{0:T(1024)S(1)} %fusion.51), kind=kCustom, calls=%fused_computation.5.clone | custom fusion | bytes 4202496 | tf_op jit(solution)/shard_map/jit(_take)/gather | solution.py:15
  455.1 3.7 fusion.30
  (59 shorter events, 2.0 us)
Async XLA Ops:
  7.2 72.4 %all-gather.20.cloned.1.call-start = ((), (), s32[]{:S(2)}) async-start(), calls=%async_computation.9 | async-start | bytes 2621440 | tf_op jit(solution)/shard_map/all_gather | solution.py:13
  11.6 5.9 %copy-start.3 = (bf16[1,4,128]{2,1,0:T(4,128)(2,1)S(1)}, bf16[1,4,128]{2,1,0:T(4,128)(2,1)}, u32[]{:S(2)}) copy-start(bf16[1,4,128]{2,1,0:T(4,128)(2,1)} %param.11) | copy-start | bytes 3076
  11.6 54.8 %copy-start.2 = (s32[1,3,2048]{2,0,1:T(1,128)S(1)}, s32[1,3,2048]{2,0,1:T(1,128)}, u32[]{:S(2)}) copy-start(s32[1,3,2048]{2,0,1:T(1,128)} %param.9) | copy-start | bytes 73732
  11.6 79.1 %all-to-all-start = ((bf16[4,512,512]{1,2,0:T(8,128)(2,1)}), bf16[4,512,512]{1,2,0:T(8,128)(2,1)S(1)}, u32[]{:S(2)}, u32[]{:S(2)}) async-start(bf16[4,512,512]{1,2,0:T(8,128)(2,1)} %stack.10), calls=%async_computation | async-start | bytes 4194304 | tf_op jit(solution)/shard_map/all_to_all | solution.py:18
  17.5 145.2 %all-gather.12.cloned.1.call-start = ((), (), s32[]{:S(2)}) async-start(), calls=%async_computation.5 | async-start | bytes 2621440 | tf_op jit(solution)/shard_map/all_gather | solution.py:13
  97.3 77.4 %all-to-all-start.1 = ((bf16[4,512,512]{1,2,0:T(8,128)(2,1)}), bf16[4,512,512]{1,2,0:T(8,128)(2,1)}, u32[]{:S(2)}, u32[]{:S(2)}) async-start(bf16[4,512,512]{1,2,0:T(8,128)(2,1)} %stack.11), calls=%async_computation.1 | async-start | bytes 4194304 | tf_op jit(solution)/shard_map/all_to_all | solution.py:18
  104.2 140.9 %all-gather.14.cloned.1.call-start = ((), (), s32[]{:S(2)}) async-start(), calls=%async_computation.6 | async-start | bytes 2621440 | tf_op jit(solution)/shard_map/all_gather | solution.py:13
  180.9 76.3 %all-to-all-start.2 = ((bf16[4,512,512]{1,2,0:T(8,128)(2,1)}), bf16[4,512,512]{1,2,0:T(8,128)(2,1)}, u32[]{:S(2)}, u32[]{:S(2)}) async-start(bf16[4,512,512]{1,2,0:T(8,128)(2,1)} %stack.12), calls=%async_computation.2 | async-start | bytes 4194304 | tf_op jit(solution)/shard_map/all_to_all | solution.py:18
  185.6 158.8 %all-gather.16.cloned.1.call-start = ((), (), s32[]{:S(2)}) async-start(), calls=%async_computation.7 | async-start | bytes 2621440 | tf_op jit(solution)/shard_map/all_gather | solution.py:13
  260.9 13.1 %collective-permute-start = (bf16[512,512]{0,1:T(8,128)(2,1)S(1)}, bf16[512,512]{0,1:T(8,128)(2,1)S(1)}, u32[]{:S(2)}, u32[]{:S(2)}) collective-permute-start(bf16[512,512]{0,1:T(8,128)(2,1)S(1)} %fusion.33), channel_id=1, source_target_pairs={{0,16},{16,32},{32,48},{48,64},{64,80},{80,96},{96,112},{112,128},... | collective-permute-start | bytes 1572872 | tf_op jit(solution)/shard_map/ppermute | solution.py:9
  274.0 0.8 copy-start
  276.3 80.1 %all-to-all-start.3 = ((bf16[4,512,512]{1,2,0:T(8,128)(2,1)}), bf16[4,512,512]{1,2,0:T(8,128)(2,1)}, u32[]{:S(2)}, u32[]{:S(2)}) async-start(bf16[4,512,512]{1,2,0:T(8,128)(2,1)} %stack.26), calls=%async_computation.3 | async-start | bytes 4194304 | tf_op jit(solution)/shard_map/all_to_all | solution.py:18
  282.2 161.8 %all-gather.18.cloned.1.call-start = ((), (), s32[]{:S(2)}) async-start(), calls=%async_computation.8 | async-start | bytes 2621440 | tf_op jit(solution)/shard_map/all_gather | solution.py:13
  285.1 5.7 %collective-permute-start.2 = (bf16[128]{0:T(256)(128)(2,1)S(1)}, bf16[128]{0:T(256)(128)(2,1)S(1)}, u32[]{:S(2)}, u32[]{:S(2)}) collective-permute-start(bf16[128]{0:T(256)(128)(2,1)S(1)} %fusion.52), channel_id=1, source_target_pairs={{0,16},{16,32},{32,48},{48,64},{64,80},{80,96},{96,112},{112,128},... | collective-permute-start | bytes 776 | tf_op jit(solution)/shard_map/ppermute | solution.py:9
  360.0 10.5 %collective-permute-start.1 = (bf16[512,512]{1,0:T(8,128)(2,1)S(1)}, bf16[512,512]{1,0:T(8,128)(2,1)S(1)}, u32[]{:S(2)}, u32[]{:S(2)}) collective-permute-start(bf16[512,512]{1,0:T(8,128)(2,1)S(1)} %fusion.24), channel_id=1, source_target_pairs={{0,32},{16,48},{32,64},{48,80},{64,96},{80,112},{96,128},{112,144}... | collective-permute-start | bytes 1572872 | tf_op jit(solution)/shard_map/ppermute | solution.py:9
  370.5 0.8 copy-start.1
  373.0 69.9 %all-to-all-start.4 = ((bf16[4,512,512]{1,2,0:T(8,128)(2,1)}), bf16[4,512,512]{1,2,0:T(8,128)(2,1)S(1)}, u32[]{:S(2)}, u32[]{:S(2)}) async-start(bf16[4,512,512]{1,2,0:T(8,128)(2,1)} %stack.27), calls=%async_computation.4 | async-start | bytes 4194304 | tf_op jit(solution)/shard_map/all_to_all | solution.py:18
  381.9 4.8 %collective-permute-start.3 = (bf16[128]{0:T(256)(128)(2,1)S(1)}, bf16[128]{0:T(256)(128)(2,1)S(1)}, u32[]{:S(2)}, u32[]{:S(2)}) collective-permute-start(bf16[128]{0:T(256)(128)(2,1)S(1)} %add_convert_fusion), channel_id=1, source_target_pairs={{0,32},{16,48},{32,64},{48,80},{64,96},{80,112},{96,128},{112,144}... | collective-permute-start | bytes 776 | tf_op jit(solution)/shard_map/ppermute | solution.py:9
Sparse Core Ops, SparseCore 0:
  10.4 32.0 all-gather.19
  94.6 30.4 all-gather.11
  179.3 29.3 all-gather.13
  274.9 29.8 all-gather.15
  371.4 29.2 all-gather.17
